TPU v7x, 512 devices: a whole 4x4x16 slice. The times are simulated.
512 devices in a mesh: row: 32 (over x, z_lo, core), col: 16 (over y, z_hi).
Axes of the slice: x: 4, y: 4, z: 16 (z_hi: 4, z_lo: 4; z = z_hi * 4 + z_lo), core: 2. Of those that a mesh axis runs over, the one named last changes fastest.
Arguments:
- hidden_img: bfloat16 [16384, 2432], P('row', 'col'), may hold values from -75 to 75
- hidden_txt: bfloat16 [3072, 2432], P('row', 'col'), may hold values from -75 to 75
- text_len: int32 [16], replicated, may hold values from 1 to 154, as said below
- step_index: int32 [16], replicated, may hold values from 0 to 27
- latent: float32 [16384, 64], P('row'), may hold values from -6 to 6
- cond: float32 [16, 2432], P(None, 'row'), may hold values from -6 to 6
- mod_weight: bfloat16 [2432, 7, 2432], P('row', None, 'col'), may hold values from -0.125 to 0.125
- qkv_weight: bfloat16 [2432, 3, 2048], P('row', None, 'col'), may hold values from -0.125 to 0.125
- kv_text_weight: bfloat16 [2432, 2, 2048], P('row', None, 'col'), may hold values from -0.125 to 0.125
- q_gain: float32 [64], replicated, may hold values from 0.5 to 6
- k_gain: float32 [2, 64], replicated, may hold values from 0.5 to 6
- out_weight: bfloat16 [2048, 2432], P('row', 'col'), may hold values from -6 to 6
- final_weight: bfloat16 [2432, 64], P('row'), may hold values from -0.125 to 0.125
Outputs:
- velocity: float32 [16384, 64], P('row')
- latent_next: float32 [16384, 64], P('row')
Inputs may be any that keep to these rules, and one draw needn't show every extreme that they name: `text_len`: some request has exactly 154 text tokens in every draw.
All inputs are finite; a program needn't handle non-finite values.
Results may differ from a plain program's by a relative error of at most 0.015.
The roundings to bfloat16 on the way count: a program that leaves them out, or rounds other values in their place, can miss the bound.
Values may be sent and summed in bfloat16 or wider, within the bound.
A program may use at most 64 MiB of HBM per device.

v0:
```python
import jax
import jax.numpy as jnp
from jax import lax
from jax.sharding import PartitionSpec as P

STEPS = 28
EPS_NORM = 1e-06


def partner_2(block, axis, distance):
    count = lax.axis_size(axis)
    route = []
    for low in range(count):
        high = low | 1 << distance
        if high != low and high < count:
            route += [(low, high), (high, low)]
    return lax.ppermute(block, axis, route)


def modulate_full(values, offset, stretch):
    average = jnp.mean(values, axis=1, keepdims=True)
    mean_square = jnp.mean(values * values, axis=1, keepdims=True)
    normed = (values - average) * lax.rsqrt(mean_square - average * average + EPS_NORM)
    return (normed * (1.0 + stretch) + offset).astype(jnp.bfloat16)


def head_norm(values, gain_row):
    mean_square = jnp.mean(values * values, axis=-1, keepdims=True)
    return (values * lax.rsqrt(mean_square + EPS_NORM) * gain_row).astype(jnp.bfloat16)


def sigma_of(step_now):
    remain = 1.0 - step_now.astype(jnp.float32) / STEPS
    return 3.0 * remain / (1.0 + 2.0 * remain)


def per_device(
    hidden_img,
    hidden_txt,
    text_len,
    step_index,
    latent,
    cond,
    mod_weight,
    qkv_weight,
    kv_text_weight,
    q_gain,
    k_gain,
    out_weight,
    final_weight,
):
    row_pos = lax.axis_index("row")
    request = row_pos // 2
    lower_half = row_pos % 2 == 0
    img_rows, width_part = hidden_img.shape
    txt_rows = hidden_txt.shape[0]
    head_dim = q_gain.shape[0]
    qkv_cols = qkv_weight.shape[2]
    heads_here = qkv_cols // head_dim
    activated = jax.nn.silu(cond).astype(jnp.bfloat16)
    mod_local = mod_weight.reshape(mod_weight.shape[0], 7 * width_part)
    mod_terms = jnp.dot(activated, mod_local, preferred_element_type=jnp.float32).reshape(
        activated.shape[0], 7, width_part
    )
    mod_all = lax.psum(mod_terms, "row")
    mod_own = lax.dynamic_index_in_dim(mod_all, request, 0, keepdims=False)
    mod_full = lax.all_gather(mod_own, "col", axis=1, tiled=True)
    img_full, txt_full = (
        lax.all_gather(hidden_img, "col", axis=1, tiled=True),
        lax.all_gather(hidden_txt, "col", axis=1, tiled=True),
    )
    img_ready = modulate_full(img_full.astype(jnp.float32), mod_full[0], mod_full[1])
    txt_ready = modulate_full(txt_full.astype(jnp.float32), mod_full[3], mod_full[4])
    qkv_flat = qkv_weight.reshape(qkv_weight.shape[0], 3 * qkv_cols)
    kv_flat = kv_text_weight.reshape(kv_text_weight.shape[0], 2 * qkv_cols)
    img_proj = jnp.dot(
        img_ready,
        lax.all_gather(qkv_flat, "row", axis=0, tiled=True),
        preferred_element_type=jnp.float32,
    )
    txt_proj = jnp.dot(
        txt_ready,
        lax.all_gather(kv_flat, "row", axis=0, tiled=True),
        preferred_element_type=jnp.float32,
    )
    img_proj = img_proj.reshape(img_rows, 3, heads_here, head_dim)
    txt_proj = txt_proj.reshape(txt_rows, 2, heads_here, head_dim)
    queries = head_norm(img_proj[:, 0], q_gain)
    img_keys = head_norm(img_proj[:, 1], k_gain[0])
    img_values = img_proj[:, 2].astype(jnp.bfloat16)
    txt_keys = head_norm(txt_proj[:, 0], k_gain[1])
    txt_values = txt_proj[:, 1].astype(jnp.bfloat16)
    length = lax.dynamic_index_in_dim(text_len, request, 0, keepdims=False)
    scaling = head_dim ** (-0.5)
    partner = partner_2((img_keys, img_values, txt_keys, txt_values), "row", 0)

    def ordered(own_part, peer_part):
        return jnp.concatenate(
            [
                jnp.where(lower_half, own_part, peer_part),
                jnp.where(lower_half, peer_part, own_part),
            ],
            axis=0,
        )

    all_keys = jnp.concatenate(
        [ordered(img_keys, partner[0]), ordered(txt_keys, partner[2])], axis=0
    )
    all_values = jnp.concatenate(
        [ordered(img_values, partner[1]), ordered(txt_values, partner[3])], axis=0
    )
    key_valid = jnp.concatenate(
        [jnp.ones((2 * img_rows,), dtype=bool), jnp.arange(2 * txt_rows) < length]
    )

    def attend(head_ops):
        q_head, k_head, v_head = head_ops
        scores = jnp.dot(q_head, k_head.T, preferred_element_type=jnp.float32) * scaling
        scores = jnp.where(key_valid[None, :], scores, -jnp.inf)
        row_max = jnp.max(scores, axis=1, keepdims=True)
        weights = jnp.exp(scores - row_max)
        probabilities = (weights / jnp.sum(weights, axis=1, keepdims=True)).astype(jnp.bfloat16)
        return jnp.dot(probabilities, v_head, preferred_element_type=jnp.float32).astype(
            jnp.bfloat16
        )

    attended = lax.map(
        attend,
        (jnp.moveaxis(queries, 1, 0), jnp.moveaxis(all_keys, 1, 0), jnp.moveaxis(all_values, 1, 0)),
    )
    attended = jnp.moveaxis(attended, 0, 1).reshape(img_rows, qkv_cols)
    full_heads = lax.all_gather(attended, "col", axis=1, tiled=True)
    projected = jnp.dot(
        full_heads,
        lax.all_gather(out_weight, "row", axis=0, tiled=True),
        preferred_element_type=jnp.float32,
    )
    updated = (hidden_img.astype(jnp.float32) + mod_own[2] * projected).astype(jnp.bfloat16)
    head_full = lax.all_gather(final_weight, "row", axis=0, tiled=True)
    residual = lax.all_gather(updated, "col", axis=1, tiled=True)
    head_in = modulate_full(residual.astype(jnp.float32), mod_full[5], mod_full[6])
    velocity = jnp.dot(head_in, head_full, preferred_element_type=jnp.float32)
    step_now = lax.dynamic_index_in_dim(step_index, request, 0, keepdims=False)
    sigma_step = sigma_of(step_now + 1) - sigma_of(step_now)
    latent_next = latent + sigma_step * velocity
    return (velocity, latent_next)


def solution(mesh):
    in_specs = (
        P("row", "col"),
        P("row", "col"),
        P(),
        P(),
        P("row", None),
        P(None, "row"),
        P("row", None, "col"),
        P("row", None, "col"),
        P("row", None, "col"),
        P(),
        P(),
        P("row", "col"),
        P("row", None),
    )
    out_specs = (P("row", None), P("row", None))
    return jax.shard_map(
        per_device, mesh=mesh, in_specs=in_specs, out_specs=out_specs, check_vma=False
    )
```

profile of v0, /device:TPU:1, one launch (start us, length us, event | category | flops | bytes accessed | tf_op | source)
XLA Modules:
  0.0 753.6 jit_solution(9680876865259763626)
XLA Ops:
  8.1 1.6 fusion.48
  9.8 1.4 reshape.166
  15.4 61.1 %all_gather.30 = bf16[96,2432]{0,1:T(8,128)(2,1)S(1)} all-gather(bf16[96,152]{0,1:T(8,128)(2,1)} %param.16), channel_id=1, replica_groups=mesh['row'=32,'col'=16] {'col'}, dimensions={1}, use_global_device_ids=true | all-gather | bytes 496128 | tf_op jit(solution)/shard_map/all_gather | solution.py:70
  78.1 199.8 %all-reduce.3.cloned.1.call-done = f32[16,7,152]{2,0,1:T(8,128)} async-done(((f32[16,7,152]{2,0,1:T(8,128)}), f32[16,7,152]{2,0,1:T(8,128)}) %all-reduce.3.cloned.1.call-update) | async-done | bytes 68112 | tf_op jit(solution)/shard_map/psum | solution.py:65
  278.8 77.3 %all-gather = f32[1,7,2432]{1,0,2:T(1,128)S(1)} all-gather(f32[1,7,152]{1,0,2:T(1,128)S(1)} %copy.52), channel_id=2, replica_groups=mesh['row'=32,'col'=16] {'col'}, dimensions={2}, use_global_device_ids=true | all-gather | bytes 72352 | tf_op jit(solution)/shard_map/all_gather | solution.py:67
  356.1 42.9 %fusion.39 = (f32[2432]{0:T(1024)}, f32[2432]{0:T(1024)S(1)}, f32[2432]{0:T(1024)S(1)}, f32[2432]{0:T(1024)}, f32[2432]{0:T(1024)}, /*index=5*/f32[2432]{0:T(1024)}) fusion(f32[1,7,2432]{1,0,2:T(1,128)S(1)} %all-gather), kind=kLoop, calls=%fused_computation.55 | loop fusion | flops 7296 | bytes 116736 | tf_op jit(solution)/shard_map/add | solution.py:24
  399.0 2.2 reshape.167
  402.4 6.7 collective-permute-start.3
  409.2 1.9 collective-permute-start.1
  413.1 14.4 %all-gather.16.cloned.1.call-done = bf16[32,76,384]{2,1,0:T(8,128)(2,1)} async-done(((bf16[1,76,384]{2,1,0:T(8,128)(2,1)}), bf16[32,76,384]{2,1,0:T(8,128)(2,1)}) %all-gather.16.cloned.1.call-update) | async-done | bytes 1867792 | tf_op jit(solution)/shard_map/all_gather | solution.py:78
  427.5 2.5 reshape.165
  429.9 103.8 %all-gather.10.cloned.1.call-done = bf16[512,2432]{0,1:T(8,128)(2,1)} async-done(((bf16[512,152]{0,1:T(8,128)(2,1)}), bf16[512,2432]{0,1:T(8,128)(2,1)}) %all-gather.10.cloned.1.call-update) | async-done | bytes 2490384 | tf_op jit(solution)/shard_map/all_gather | solution.py:69
  533.7 2.6 convert_reduce_fusion.1
  536.4 1.9 fusion.24
  538.5 2.8 collective-permute-start
  541.3 2.1 collective-permute-start.2
  544.9 3.1 while.10
  548.7 44.3 %all_gather.33 = bf16[2048,152]{1,0:T(8,128)(2,1)S(1)} all-gather(bf16[64,152]{1,0:T(8,128)(2,1)S(1)} %copy-done.6), channel_id=1, replica_groups=mesh['row'=32,'col'=16] {'row'}, dimensions={0}, use_global_device_ids=true | all-gather | bytes 642048 | tf_op jit(solution)/shard_map/all_gather | solution.py:135
  593.8 45.6 %all-gather.12.cloned.1.call-done = bf16[512,2048]{0,1:T(8,128)(2,1)} async-done(((bf16[512,128]{0,1:T(8,128)(2,1)}), bf16[512,2048]{0,1:T(8,128)(2,1)}) %all-gather.12.cloned.1.call-update) | async-done | bytes 2097168 | tf_op jit(solution)/shard_map/all_gather | solution.py:132
  639.4 2.8 fusion.41
  644.2 45.2 %all-gather.3 = bf16[32,76,64]{1,2,0:T(8,128)(2,1)S(1)} all-gather(bf16[1,76,64]{1,2,0:T(8,128)(2,1)S(1)} %bitcast.104), channel_id=1, replica_groups=mesh['row'=32,'col'=16] {'row'}, dimensions={0}, use_global_device_ids=true | all-gather | bytes 321024 | tf_op jit(solution)/shard_map/all_gather | solution.py:139
  690.6 51.6 %all-gather.14.cloned.1.call-done = bf16[512,2432]{0,1:T(8,128)(2,1)} async-done(((bf16[512,152]{0,1:T(8,128)(2,1)}), bf16[512,2432]{0,1:T(8,128)(2,1)}) %all-gather.14.cloned.1.call-update) | async-done | bytes 2490384 | tf_op jit(solution)/shard_map/all_gather | solution.py:140
  742.3 2.6 convert_reduce_fusion
  744.9 1.8 multiply_add_fusion
  (87 shorter events, 18.7 us)
Async XLA Ops:
  7.2 270.7 %all-reduce.3.cloned.1.call-start = ((), (), s32[]{:S(2)}) async-start(), calls=%async_computation | async-start | bytes 229376 | tf_op jit(solution)/shard_map/psum | solution.py:65
  9.8 389.2 %all-gather.18.cloned.1.call-start = ((), (), s32[]{:S(2)}) async-start(), calls=%async_computation.5 | async-start | bytes 1351680 | tf_op jit(solution)/shard_map/all_gather | solution.py:83
  11.3 416.2 %all-gather.16.cloned.1.call-start = ((), (), s32[]{:S(2)}) async-start(), calls=%async_computation.4 | async-start | bytes 2027520 | tf_op jit(solution)/shard_map/all_gather | solution.py:78
  12.9 520.9 %all-gather.10.cloned.1.call-start = ((), (), s32[]{:S(2)}) async-start(), calls=%async_computation.1 | async-start | bytes 2646016 | tf_op jit(solution)/shard_map/all_gather | solution.py:69
  13.5 626.0 %all-gather.12.cloned.1.call-start = ((), (), s32[]{:S(2)}) async-start(), calls=%async_computation.2 | async-start | bytes 2228224 | tf_op jit(solution)/shard_map/all_gather | solution.py:132
  402.4 8.8 %collective-permute-start.3 = (bf16[96,2,64]{0,2,1:T(8,128)(2,1)S(1)}, bf16[96,2,64]{0,2,1:T(8,128)(2,1)S(1)}, u32[]{:S(2)}, u32[]{:S(2)}) collective-permute-start(bf16[96,2,64]{0,2,1:T(8,128)(2,1)S(1)} %fusion.52), channel_id=1, source_target_pairs={{0,16},{16,0},{32,48},{48,32},{64,80},{80,64},{96,112},{112,96},{1... | collective-permute-start | bytes 73736 | tf_op jit(solution)/shard_map/ppermute | solution.py:17
  409.2 3.1 collective-permute-start.1
  413.1 123.3 %copy-start.10 = (f32[2432]{0:T(1024)S(1)}, f32[2432]{0:T(1024)}, u32[]{:S(2)}) copy-start(f32[2432]{0:T(1024)} %get-tuple-element.48) | copy-start | bytes 29188
  413.1 123.3 %copy-start.11 = (f32[2432]{0:T(1024)S(1)}, f32[2432]{0:T(1024)}, u32[]{:S(2)}) copy-start(f32[2432]{0:T(1024)} %get-tuple-element.49) | copy-start | bytes 29188
  533.7 2.6 copy-start.1
  536.3 2.0 copy-start.12
  536.3 2.0 copy-start.13
  538.2 6.5 copy-start.5
  538.5 5.0 collective-permute-start
  541.3 3.4 collective-permute-start.2
  544.9 3.8 copy-start.6
  544.9 94.5 %copy-start.3 = (bf16[512,152]{0,1:T(8,128)(2,1)S(1)}, bf16[512,152]{0,1:T(8,128)(2,1)}, u32[]{:S(2)}) copy-start(bf16[512,152]{0,1:T(8,128)(2,1)} %param.15) | copy-start | bytes 466948
  548.0 94.3 %copy-start.15 = (s32[16]{0:T(128)S(1)}, s32[16]{0:T(128)}, u32[]{:S(2)}) copy-start(s32[16]{0:T(128)} %param.18) | copy-start | bytes 196
  548.0 96.2 %copy-start.7 = (bf16[76,64]{0,1:T(8,128)(2,1)S(1)}, bf16[76,64]{0,1:T(8,128)(2,1)}, u32[]{:S(2)}) copy-start(bf16[76,64]{0,1:T(8,128)(2,1)} %param.27) | copy-start | bytes 29188
  548.7 193.6 %all-gather.14.cloned.1.call-start = ((), (), s32[]{:S(2)}) async-start(), calls=%async_computation.3 | async-start | bytes 2646016 | tf_op jit(solution)/shard_map/all_gather | solution.py:140
  642.3 102.6 %copy-start.8 = (f32[2432]{0:T(1024)S(1)}, f32[2432]{0:T(1024)}, u32[]{:S(2)}) copy-start(f32[2432]{0:T(1024)} %get-tuple-element.45) | copy-start | bytes 29188
  642.3 102.6 %copy-start.9 = (f32[2432]{0:T(1024)S(1)}, f32[2432]{0:T(1024)}, u32[]{:S(2)}) copy-start(f32[2432]{0:T(1024)} %get-tuple-element.50) | copy-start | bytes 29188
  642.3 102.6 %copy-start.14 = (f32[512,64]{0,1:T(8,128)S(1)}, f32[512,64]{0,1:T(8,128)}, u32[]{:S(2)}) copy-start(f32[512,64]{0,1:T(8,128)} %param.19) | copy-start | bytes 393220
  742.3 2.6 copy-start.2
  (2 other events, 1.6 us)
Sparse Core Ops, SparseCore 0:
  11.5 266.3 all-reduce.2
  280.2 76.0 all-gather.17
  359.3 68.1 all-gather.15
  430.8 102.8 all-gather.9
  548.8 90.5 all-gather.11
  642.8 99.4 all-gather.13
where the time goes:
time: 754 us
  waiting for transfers between devices  417 us (55%)
  blocking collectives  228 us (30%)
  other arithmetic  51.4 us (7%)
  local copies, waits for them, and re-layouts  16 us (2%)
  between operations  15.9 us (2%)
  starting transfers between devices  13.8 us (2%)
  matrix products  11.6 us (2%)
    psum x1, waiting for transfers between devices, per_device(): mod_all = lax.psum(mod_terms, 'row')  200 us
    all_gather x1, waiting for transfers between devices, per_device(): lax.all_gather(hidden_img, 'col', axis=1, tiled=True)  104 us
    all_gather x1, blocking collectives, per_device(): mod_full = lax.all_gather(mod_own, 'col', axis=1, tiled=True)  77.3 us
    all_gather x1, blocking collectives, per_device(): lax.all_gather(hidden_txt, 'col', axis=1, tiled=True)  61.1 us
    all_gather x1, waiting for transfers between devices, per_device(): residual = lax.all_gather(updated, 'col', axis=1, tiled=True)  51.6 us
    all_gather x1, waiting for transfers between devices, per_device(): full_heads = lax.all_gather(attended, 'col', axis=1, tiled=True)  45.6 us
    all_gather x1, blocking collectives, per_device(): head_full = lax.all_gather(final_weight, 'row', axis=0, tiled=True)  45.2 us
    all_gather x1, blocking collectives, per_device(): lax.all_gather(out_weight, 'row', axis=0, tiled=True)  44.3 us
  transfers between devices with their start and end apart: 10, of which 7 were waited for; matrix products, arithmetic and copies ran while one was open for 8% of the time, Pallas kernels for 0%

commit v1 on v0

--- a/solution.py
+++ b/solution.py
@@ -66,7 +66,9 @@
     mod_own = lax.dynamic_index_in_dim(mod_all, request, 0, keepdims=False)
     mod_full = lax.all_gather(mod_own, "col", axis=1, tiled=True)
     img_full, txt_full = (
-        lax.all_gather(hidden_img, "col", axis=1, tiled=True),
+        jnp.concatenate(
+            lax.all_to_all(jnp.stack([hidden_img] * lax.axis_size("col")), "col", 0, 0), axis=1
+        ),
         lax.all_gather(hidden_txt, "col", axis=1, tiled=True),
     )
     img_ready = modulate_full(img_full.astype(jnp.float32), mod_full[0], mod_full[1])

time: 754 us -> 718 us (0.952)
  waiting for transfers between devices: 417 us -> 268 us
  blocking collectives: 228 us -> 322 us
  starting transfers between devices: 13.8 us -> 31.9 us
    all_gather x1 -> x0, waiting for transfers between devices: 104 us -> none  [per_device(): lax.all_gather(hidden_img, 'col', axis=1, tiled=True)]
    all_gather x1, blocking collectives: 61.1 us -> 151 us  [per_device(): lax.all_gather(hidden_txt, 'col', axis=1, tiled=True)]
    psum x1, waiting for transfers between devices: 200 us -> 156 us  [per_device(): mod_all = lax.psum(mod_terms, 'row')]
    all_to_all x0 -> x1, starting transfers between devices: none -> 18.5 us  [per_device(): lax.all_to_all(jnp.stack([hidden_img] * lax.axis_size('col')), 'col', 0, 0)]
  transfers between devices with their start and end apart: 10 -> 10, of which waited for: 7 -> 6; matrix products, arithmetic and copies ran while one was open for 8% -> 9% of each run, Pallas kernels for 0% -> 0%
where the time goes in v1:
time: 718 us
  blocking collectives  322 us (45%)
  waiting for transfers between devices  268 us (37%)
  other arithmetic  49.1 us (7%)
  starting transfers between devices  31.9 us (4%)
  local copies, waits for them, and re-layouts  20.1 us (3%)
  between operations  15.7 us (2%)
  matrix products  11.5 us (2%)
    psum x1, waiting for transfers between devices, per_device(): mod_all = lax.psum(mod_terms, 'row')  156 us
    all_gather x1, blocking collectives, per_device(): lax.all_gather(hidden_txt, 'col', axis=1, tiled=True)  151 us
    all_gather x1, blocking collectives, per_device(): mod_full = lax.all_gather(mod_own, 'col', axis=1, tiled=True)  77.3 us
    all_gather x1, waiting for transfers between devices, per_device(): residual = lax.all_gather(updated, 'col', axis=1, tiled=True)  51.2 us
    all_gather x1, blocking collectives, per_device(): lax.all_gather(out_weight, 'row', axis=0, tiled=True)  47.4 us
    all_gather x1, waiting for transfers between devices, per_device(): full_heads = lax.all_gather(attended, 'col', axis=1, tiled=True)  46 us
    all_gather x1, blocking collectives, per_device(): head_full = lax.all_gather(final_weight, 'row', axis=0, tiled=True)  45.9 us
    add x1, other arithmetic, modulate_full(): return (normed * (1.0 + stretch) + offset).astype(jnp.bfloat16)  42.5 us
  transfers between devices with their start and end apart: 10, of which 6 were waited for; matrix products, arithmetic and copies ran while one was open for 9% of the time, Pallas kernels for 0%

profile of v1, /device:TPU:1, one launch (start us, length us, event | category | flops | bytes accessed | tf_op | source)
XLA Modules:
  0.0 717.7 jit_solution(12694141570608553148)
XLA Ops:
  7.2 2.6 stack.2
  9.8 18.5 %all-to-all-start = ((bf16[16,512,152]{1,2,0:T(8,128)(2,1)}), bf16[16,512,152]{1,2,0:T(8,128)(2,1)S(1)}, u32[]{:S(2)}, u32[]{:S(2)}) async-start(bf16[16,512,152]{1,2,0:T(8,128)(2,1)} %stack.2), calls=%async_computation | async-start | bytes 4980736 | tf_op jit(solution)/shard_map/all_to_all | solution.py:70
  32.4 151.0 %all_gather.26 = bf16[96,2432]{0,1:T(8,128)(2,1)S(1)} all-gather(bf16[96,152]{0,1:T(8,128)(2,1)S(1)} %copy-done.7), channel_id=1, replica_groups=mesh['row'=32,'col'=16] {'col'}, dimensions={1}, use_global_device_ids=true | all-gather | bytes 496128 | tf_op jit(solution)/shard_map/all_gather | solution.py:72
  183.7 156.1 %all-reduce.3.cloned.1.call-done = f32[16,7,152]{2,0,1:T(8,128)} async-done(((f32[16,7,152]{2,0,1:T(8,128)}), f32[16,7,152]{2,0,1:T(8,128)}) %all-reduce.3.cloned.1.call-update) | async-done | bytes 68112 | tf_op jit(solution)/shard_map/psum | solution.py:65
  340.7 77.3 %all-gather = f32[1,7,2432]{1,0,2:T(1,128)S(1)} all-gather(f32[1,7,152]{1,0,2:T(1,128)S(1)} %copy.37), channel_id=2, replica_groups=mesh['row'=32,'col'=16] {'col'}, dimensions={2}, use_global_device_ids=true | all-gather | bytes 72352 | tf_op jit(solution)/shard_map/all_gather | solution.py:67
  418.0 42.5 %fusion.33 = (f32[2432]{0:T(1024)S(1)}, f32[2432]{0:T(1024)S(1)}, f32[2432]{0:T(1024)S(1)}, f32[2432]{0:T(1024)S(1)}, f32[2432]{0:T(1024)S(1)}, /*index=5*/f32[2432]{0:T(1024)S(1)}) fusion(f32[1,7,2432]{1,0,2:T(1,128)S(1)} %all-gather), kind=kLoop, calls=%fused_computation.50 | loop fusion | flops 7296 | bytes 116736 | tf_op jit(solution)/shard_map/add | solution.py:24
  460.7 2.9 reshape.190
  463.7 2.5 fusion.36
  466.3 6.7 collective-permute-start.3
  473.1 2.1 collective-permute-start.1
  476.3 12.6 %all-gather.13.cloned.1.call-done = bf16[32,76,384]{2,1,0:T(8,128)(2,1)} async-done(((bf16[1,76,384]{2,1,0:T(8,128)(2,1)}), bf16[32,76,384]{2,1,0:T(8,128)(2,1)}) %all-gather.13.cloned.1.call-update) | async-done | bytes 1867792 | tf_op jit(solution)/shard_map/all_gather | solution.py:80
  488.9 3.7 reshape.188
  492.6 3.9 copy.39
  498.7 1.2 fusion.50
  500.0 2.2 collective-permute-start.2
  502.3 2.1 collective-permute-start
  505.7 3.1 while.10
  509.6 47.4 %all_gather.29 = bf16[2048,152]{1,0:T(8,128)(2,1)S(1)} all-gather(bf16[64,152]{1,0:T(8,128)(2,1)S(1)} %copy-done.9), channel_id=1, replica_groups=mesh['row'=32,'col'=16] {'row'}, dimensions={0}, use_global_device_ids=true | all-gather | bytes 642048 | tf_op jit(solution)/shard_map/all_gather | solution.py:137
  557.7 46.0 %all-gather.9.cloned.1.call-done = bf16[512,2048]{0,1:T(8,128)(2,1)} async-done(((bf16[512,128]{0,1:T(8,128)(2,1)}), bf16[512,2048]{0,1:T(8,128)(2,1)}) %all-gather.9.cloned.1.call-update) | async-done | bytes 2097168 | tf_op jit(solution)/shard_map/all_gather | solution.py:134
  603.7 2.8 fusion.35
  608.5 45.9 %all-gather.3 = bf16[32,76,64]{1,2,0:T(8,128)(2,1)S(1)} all-gather(bf16[1,76,64]{1,2,0:T(8,128)(2,1)S(1)} %bitcast.110), channel_id=1, replica_groups=mesh['row'=32,'col'=16] {'row'}, dimensions={0}, use_global_device_ids=true | all-gather | bytes 321024 | tf_op jit(solution)/shard_map/all_gather | solution.py:141
  655.6 51.2 %all-gather.11.cloned.1.call-done = bf16[512,2432]{0,1:T(8,128)(2,1)} async-done(((bf16[512,152]{0,1:T(8,128)(2,1)}), bf16[512,2432]{0,1:T(8,128)(2,1)}) %all-gather.11.cloned.1.call-update) | async-done | bytes 2490384 | tf_op jit(solution)/shard_map/all_gather | solution.py:142
  706.8 2.6 convert_reduce_fusion
  709.4 1.8 multiply_add_fusion
  (93 shorter events, 16.4 us)
Async XLA Ops:
  7.2 21.2 %copy-start = (bf16[76,7,152]{0,2,1:T(8,128)(2,1)S(1)}, bf16[76,7,152]{0,2,1:T(8,128)(2,1)}, u32[]{:S(2)}) copy-start(bf16[76,7,152]{0,2,1:T(8,128)(2,1)} %param.21) | copy-start | bytes 485188
  9.7 18.6 %copy-start.11 = (f32[16,76]{1,0:T(8,128)S(1)}, f32[16,76]{1,0:T(8,128)}, u32[]{:S(2)}) copy-start(f32[16,76]{1,0:T(8,128)} %param.20) | copy-start | bytes 14596
  9.7 19.6 %copy-start.8 = (bf16[76,2,128]{2,1,0:T(2,128)(2,1)S(1)}, bf16[76,2,128]{2,1,0:T(2,128)(2,1)}, u32[]{:S(2)}) copy-start(bf16[76,2,128]{2,1,0:T(2,128)(2,1)} %param.23) | copy-start | bytes 116740
  9.7 20.4 %copy-start.6 = (bf16[76,3,128]{2,0,1:T(8,128)(2,1)S(1)}, bf16[76,3,128]{2,0,1:T(8,128)(2,1)}, u32[]{:S(2)}) copy-start(bf16[76,3,128]{2,0,1:T(8,128)(2,1)} %param.22) | copy-start | bytes 175108
  9.7 21.2 %copy-start.15 = (s32[16]{0:T(128)S(1)}, s32[16]{0:T(128)}, u32[]{:S(2)}) copy-start(s32[16]{0:T(128)} %param.17) | copy-start | bytes 196
  9.8 22.6 %copy-start.7 = (bf16[96,152]{0,1:T(8,128)(2,1)S(1)}, bf16[96,152]{0,1:T(8,128)(2,1)}, u32[]{:S(2)}) copy-start(bf16[96,152]{0,1:T(8,128)(2,1)} %param.16) | copy-start | bytes 87556
  9.8 173.9 %copy-start.12 = (f32[2,64]{1,0:T(2,128)S(1)}, f32[2,64]{1,0:T(2,128)}, u32[]{:S(2)}) copy-start(f32[2,64]{1,0:T(2,128)} %param.25) | copy-start | bytes 1540
  9.8 486.7 %all-to-all-start = ((bf16[16,512,152]{1,2,0:T(8,128)(2,1)}), bf16[16,512,152]{1,2,0:T(8,128)(2,1)S(1)}, u32[]{:S(2)}, u32[]{:S(2)}) async-start(bf16[16,512,152]{1,2,0:T(8,128)(2,1)} %stack.2), calls=%async_computation | async-start | bytes 4980736 | tf_op jit(solution)/shard_map/all_to_all | solution.py:70
  28.3 311.5 %all-reduce.3.cloned.1.call-start = ((), (), s32[]{:S(2)}) async-start(), calls=%async_computation.1 | async-start | bytes 229376 | tf_op jit(solution)/shard_map/psum | solution.py:65
  29.3 431.4 %all-gather.15.cloned.1.call-start = ((), (), s32[]{:S(2)}) async-start(), calls=%async_computation.5 | async-start | bytes 1351680 | tf_op jit(solution)/shard_map/all_gather | solution.py:85
  30.1 458.8 %all-gather.13.cloned.1.call-start = ((), (), s32[]{:S(2)}) async-start(), calls=%async_computation.4 | async-start | bytes 2027520 | tf_op jit(solution)/shard_map/all_gather | solution.py:80
  30.9 572.8 %all-gather.9.cloned.1.call-start = ((), (), s32[]{:S(2)}) async-start(), calls=%async_computation.2 | async-start | bytes 2228224 | tf_op jit(solution)/shard_map/all_gather | solution.py:134
  466.3 8.9 %collective-permute-start.3 = (bf16[96,2,64]{0,2,1:T(8,128)(2,1)S(1)}, bf16[96,2,64]{0,2,1:T(8,128)(2,1)S(1)}, u32[]{:S(2)}, u32[]{:S(2)}) collective-permute-start(bf16[96,2,64]{0,2,1:T(8,128)(2,1)S(1)} %fusion.46), channel_id=1, source_target_pairs={{0,16},{16,0},{32,48},{48,32},{64,80},{80,64},{96,112},{112,96},{1... | collective-permute-start | bytes 73736 | tf_op jit(solution)/shard_map/ppermute | solution.py:17
  473.1 3.1 collective-permute-start.1
  498.7 3.5 copy-start.13
  499.9 5.8 copy-start.4
  500.0 4.5 collective-permute-start.2
  502.3 3.2 collective-permute-start
  505.7 3.8 copy-start.9
  505.7 98.0 %copy-start.3 = (bf16[512,152]{0,1:T(8,128)(2,1)S(1)}, bf16[512,152]{0,1:T(8,128)(2,1)}, u32[]{:S(2)}) copy-start(bf16[512,152]{0,1:T(8,128)(2,1)} %param.15) | copy-start | bytes 466948
  508.8 97.7 %copy-start.16 = (s32[16]{0:T(128)S(1)}, s32[16]{0:T(128)}, u32[]{:S(2)}) copy-start(s32[16]{0:T(128)} %param.18) | copy-start | bytes 196
  508.9 99.6 %copy-start.10 = (bf16[76,64]{0,1:T(8,128)(2,1)S(1)}, bf16[76,64]{0,1:T(8,128)(2,1)}, u32[]{:S(2)}) copy-start(bf16[76,64]{0,1:T(8,128)(2,1)} %param.27) | copy-start | bytes 29188
  509.5 197.3 %all-gather.11.cloned.1.call-start = ((), (), s32[]{:S(2)}) async-start(), calls=%async_computation.3 | async-start | bytes 2646016 | tf_op jit(solution)/shard_map/all_gather | solution.py:142
  606.5 102.8 %copy-start.14 = (f32[512,64]{0,1:T(8,128)S(1)}, f32[512,64]{0,1:T(8,128)}, u32[]{:S(2)}) copy-start(f32[512,64]{0,1:T(8,128)} %param.19) | copy-start | bytes 393220
  (3 other events, 4.8 us)
Sparse Core Ops, SparseCore 0:
  32.6 307.1 all-reduce.2
  342.2 76.0 all-gather.14
  420.6 68.2 all-gather.12
  509.6 94.0 all-gather.8
  607.0 99.7 all-gather.10
